TPU v7x, 32 devices: a whole 2x2x4 slice. The times are simulated.
32 devices in a mesh: groups: 2 (over y), segment: 4 (over z), inner: 4 (over x, core).
Axes of the slice: x: 2, y: 2, z: 4, core: 2. Of those that a mesh axis runs over, the one named last changes fastest.
Arguments:
- tokens: int32 [3, 64], P(None, 'groups'), parts along dimension 1, may hold values from 0 to 511
- embedding: bfloat16 [512, 4096], P(None, 'inner'), may hold values from -6 to 6
- in_proj: bfloat16 [4, 3, 4096, 4096], P('segment', None, None, 'inner'), may hold values from -0.09375 to 0.09375
- out_proj: bfloat16 [4, 4096, 4096], P('segment', 'inner'), may hold values from -0.09375 to 0.09375
- norm_gain: float32 [4, 4096], P('segment'), may hold values from 0.1 to 1.9
- fir_taps: float32 [4, 7, 4096], P('segment', None, 'inner'), may hold values from -2 to 2
- modal_rate: float32 [4, 8, 4096], P('segment', None, 'inner'), may hold values from 0.05 to 3
- modal_residue: float32 [4, 8, 4096], P('segment', None, 'inner'), may hold values from -2 to 2
- fir_state: float32 [4, 64, 6, 4096], P('segment', 'groups', None, 'inner'), parts along dimension 1, may hold values from -6 to 6
- modal_state: float32 [4, 64, 8, 4096], P('segment', 'groups', None, 'inner'), parts along dimension 1, may hold values from -6 to 6
- final_gain: float32 [4096], replicated, may hold values from 0.1 to 1.9
- unembed: bfloat16 [4096, 512], P(None, 'inner'), may hold values from -0.25 to 0.25
Outputs:
- logits: float32 [2, 64, 512], P(None, ('groups', 'segment'), 'inner'), parts along dimension 1
- logprob: float32 [2, 64], P(None, ('groups', 'segment')), parts along dimension 1
- fir_state_out: float32 [4, 64, 6, 4096], P('segment', 'groups', None, 'inner'), parts along dimension 1
- modal_state_out: float32 [4, 64, 8, 4096], P('segment', 'groups', None, 'inner'), parts along dimension 1
There are 2 independent parts, one for each index of `groups`. A program takes and returns all parts, laid end to end along the dimension named above; an argument that names none is the same for every part. Nothing has to cross between parts.
All inputs are finite; a program needn't handle non-finite values.
Results may differ from a plain program's by a relative error of at most 0.025.
Values may be sent and summed in bfloat16 or wider, within the bound.
No kernel may reach another device: no remote copies, remote signals or barrier semaphores. Data moves between devices by JAX's collectives and lax.ppermute only.
A program may use at most 128 MiB of HBM per device.

v0:
```python
import jax
import jax.numpy as jnp
from jax import lax
from jax.sharding import PartitionSpec as P

MICRO = 2


def from_behind(block, axis, distance):
    devices = range(lax.axis_size(axis))
    route = [(i - distance, i) for i in devices if i - distance in devices]
    return lax.ppermute(block, axis, route)


def normed(values, scale_gain):
    mean_square = jnp.mean(values * values, axis=-1, keepdims=True)
    return values * lax.rsqrt(mean_square + 1e-05) * scale_gain


def short_filter(operands):
    product, fir_rows, modal_rows, taps_local, rate_local, residue_local = operands
    window = jnp.concatenate([fir_rows, product[:, None, :]], axis=1)
    filtered = jnp.sum(window * taps_local[::-1][None], axis=1)
    return (filtered, window[:, 1:], modal_rows)


def modal_filter(operands):
    product, fir_rows, modal_rows, taps_local, rate_local, residue_local = operands
    decay_factor = jnp.exp(-rate_local)
    mode_values = decay_factor[None] * modal_rows + (1.0 - decay_factor[None]) * product[:, None, :]
    filtered = jnp.sum(residue_local[None] * mode_values, axis=1) + taps_local[0][None] * product
    return (filtered, fir_rows, mode_values)


def per_device(
    tokens,
    embedding,
    in_proj,
    out_proj,
    norm_gain,
    fir_taps,
    modal_rate,
    modal_residue,
    fir_state,
    modal_state,
    final_gain,
    unembed,
):
    segment_count = lax.axis_size("segment")
    segment_index = lax.axis_index("segment")
    inner_index = lax.axis_index("inner")
    step_count = tokens.shape[0] - 1
    seq_count = tokens.shape[1]
    block_count = MICRO
    row_count = seq_count // block_count
    item_count = step_count * block_count
    tick_count = item_count + segment_count - 1
    local_width = embedding.shape[1]
    w_in = in_proj[0]
    w_out = out_proj[0]
    gain_local = norm_gain[0]
    taps_local = fir_taps[0]
    rate_local = modal_rate[0]
    residue_local = modal_residue[0]
    is_short = segment_index % 2 == 0
    is_last = segment_index == segment_count - 1

    def advance(carry, tick_index):
        previous, fir_all, modal_all, recorded = carry
        item_index = tick_index - segment_index
        is_valid = (item_index >= 0) & (item_index < item_count)
        clipped = jnp.clip(item_index, 0, item_count - 1)
        step_index = clipped // block_count
        row_start = clipped % block_count * row_count
        incoming = from_behind(previous, "segment", 1)
        token_ids = lax.dynamic_slice(tokens, (step_index, row_start), (1, row_count))[0]
        looked_up = jnp.take(embedding, token_ids, axis=0)
        stream_in = jnp.where(segment_index == 0, looked_up, incoming)
        gathered = lax.all_gather(stream_in, "inner", axis=1, tiled=True)
        normalized = normed(gathered.astype(jnp.float32), gain_local).astype(jnp.bfloat16)
        projected = jnp.einsum("bd,jdc->jbc", normalized, w_in, preferred_element_type=jnp.float32)
        product = projected[1] * projected[2]
        fir_rows = lax.dynamic_slice_in_dim(fir_all, row_start, row_count, 0)
        modal_rows = lax.dynamic_slice_in_dim(modal_all, row_start, row_count, 0)
        filtered, fir_next, modal_next = lax.cond(
            is_short,
            short_filter,
            modal_filter,
            (product, fir_rows, modal_rows, taps_local, rate_local, residue_local),
        )
        fir_all = lax.dynamic_update_slice_in_dim(
            fir_all, jnp.where(is_valid, fir_next, fir_rows), row_start, 0
        )
        modal_all = lax.dynamic_update_slice_in_dim(
            modal_all, jnp.where(is_valid, modal_next, modal_rows), row_start, 0
        )
        gated_rows = (projected[0] * filtered).astype(jnp.bfloat16)
        partial_sum = jnp.dot(gated_rows, w_out, preferred_element_type=jnp.float32)
        mixed_sum = lax.psum_scatter(partial_sum, "inner", scatter_dimension=1, tiled=True)
        stream_out = (stream_in.astype(jnp.float32) + mixed_sum).astype(jnp.bfloat16)
        current = lax.dynamic_slice(
            recorded, (step_index, row_start, jnp.int32(0)), (1, row_count, local_width)
        )
        recorded = lax.dynamic_update_slice(
            recorded,
            jnp.where(is_valid & is_last, stream_out[None], current),
            (step_index, row_start, jnp.int32(0)),
        )
        return ((stream_out, fir_all, modal_all, recorded), None)

    initial = (
        jnp.zeros((row_count, local_width), jnp.bfloat16),
        fir_state[0],
        modal_state[0],
        jnp.zeros((step_count, seq_count, local_width), jnp.bfloat16),
    )
    final_carry, unused = lax.scan(advance, initial, jnp.arange(tick_count, dtype=jnp.int32))
    last_out, fir_final, modal_final, recorded = final_carry
    final_stream = lax.all_gather(recorded, "inner", axis=2, tiled=True)
    head_in = normed(final_stream.astype(jnp.float32), final_gain).astype(jnp.bfloat16)
    logits = jnp.einsum("tsd,dv->tsv", head_in, unembed, preferred_element_type=jnp.float32)
    vocab_local = unembed.shape[1]
    columns = inner_index * vocab_local + jnp.arange(vocab_local, dtype=jnp.int32)
    targets = tokens[1:]
    exp_local = jnp.sum(jnp.exp(logits), axis=-1)
    target_part = jnp.sum(
        jnp.where(columns[None, None, :] == targets[:, :, None], logits, 0.0), axis=-1
    )
    exp_total, target_logit = lax.psum((exp_local, target_part), "inner")
    logprob = target_logit - jnp.log(exp_total)
    logits_kept = jnp.where(is_last, logits, 0.0)
    logprob_kept = jnp.where(is_last, logprob, 0.0)
    logits_out, logprob_out = (
        lax.psum_scatter(logits_kept, "segment", scatter_dimension=1, tiled=True),
        lax.psum_scatter(logprob_kept, "segment", scatter_dimension=1, tiled=True),
    )
    return (logits_out, logprob_out, fir_final[None], modal_final[None])


def solution(mesh):
    return jax.shard_map(
        per_device,
        mesh=mesh,
        in_specs=(
            P(None, "groups"),
            P(None, "inner"),
            P("segment", None, None, "inner"),
            P("segment", "inner", None),
            P("segment", None),
            P("segment", None, "inner"),
            P("segment", None, "inner"),
            P("segment", None, "inner"),
            P("segment", "groups", None, "inner"),
            P("segment", "groups", None, "inner"),
            P(),
            P(None, "inner"),
        ),
        out_specs=(
            P(None, ("groups", "segment"), "inner"),
            P(None, ("groups", "segment")),
            P("segment", "groups", None, "inner"),
            P("segment", "groups", None, "inner"),
        ),
        check_vma=False,
    )
```

profile of v0, /device:TPU:0, one launch (start us, length us, event | category | flops | bytes accessed | tf_op | source)
XLA Modules:
  0.0 421.6 jit_solution(7223854443020577943)
XLA Ops:
  8.0 2.4 copy.56
  10.4 2.6 copy.26
  14.5 369.0 %while.19 = (s32[]{:T(128)}, bf16[16,1024]{1,0:T(8,128)(2,1)S(1)}, f32[32,6,1024]{2,1,0:T(8,128)}, f32[32,8,1024]{2,1,0:T(8,128)}, bf16[2,32,1024]{2,1,0:T(8,128...) while((s32[]{:T(128)}, bf16[16,1024]{1,0:T(8,128)(2,1)S(1)}, ...), condition=%wide.region_7.8_spmd.clone, body=%wide.region_0.7_spmd.clone.sunk | while | flops 538412224 | bytes 43820432 | solution.py:117
  14.6 5.0 %collective-permute-start = (bf16[16,1024]{1,0:T(8,128)(2,1)S(1)}, bf16[16,1024]{1,0:T(8,128)(2,1)S(1)}, u32[]{:S(2)}, u32[]{:S(2)}) collective-permute-start(bf16[16,1024]{1,0:T(8,128)(2,1)S(1)} %broadcast_select_fusion.3), channel_id=1, source_target_pairs={{0,4},{4,8},{8,12},{1,5},{5,9},{9,13},{2,6},{6,10},{10,14},{3,7},{... | collective-permute-start | bytes 98312 | tf_op jit(solution)/shard_map/while/body/eval_jaxpr/ppermute | solution.py:12
  24.5 2.0 gather_fusion
  26.6 5.4 %all_gather.12 = bf16[16,4096]{1,0:T(8,128)(2,1)S(1)} all-gather(bf16[16,1024]{1,0:T(8,128)(2,1)S(1)} %select_select_fusion.2), channel_id=1, replica_groups=mesh['groups'=2,'segment'=4,'inner'=4] {'inner'}, dimensions={1}, use_global_device_ids=true | all-gather | bytes 163840 | tf_op jit(solution)/shard_map/while/body/eval_jaxpr/all_gather | solution.py:79
  32.2 10.0 %convolution_bitcast_fusion.2 = f32[3,16,1024]{2,1,0:T(8,128)S(1)} fusion(bf16[3,4096,1024]{2,1,0:T(8,128)(2,1)} %get-tuple-element.555, bf16[16,4096]{1,0:T(8,128)(2,1)S(1)} %all_gather.12, f32[4096]{0:T(1024)} %bitcast.78, f32[16]{0:T(128)S(1)} %add_rsqrt_fusion.3), kind=kOutput, calls=%fused_computation.11.clone.1 | convolution fusion | flops 402915328 | bytes 25509952 | tf_op jit(solution)/shard_map/while/body/eval_jaxpr/bd,jdc->jbc/dot_general | solution.py:81
  42.9 5.3 %fusion.43 = f32[16,4096]{1,0:T(8,128)} fusion(bf16[1024,4096]{1,0:T(8,128)(2,1)} %get-tuple-element.560, f32[16,1024]{1,0:T(8,128)S(1)} %get-tuple-element.481, f32[3,16,1024]{2,1,0:T(8,128)S(1)} %convolution_bitcast_fusion.2), kind=kOutput, calls=%fused_computation.28.clone.1 | convolution fusion | flops 134250496 | bytes 8781824 | tf_op jit(solution)/shard_map/while/body/eval_jaxpr/dot_general | solution.py:98
  52.0 16.6 %reduce-scatter.6.cloned.1.call-done = f32[16,1024]{1,0:T(8,128)} async-done(((f32[16,4096]{1,0:T(8,128)}), f32[16,1024]{1,0:T(8,128)}) %reduce-scatter.6.cloned.1.call-update) | async-done | bytes 65552 | tf_op jit(solution)/shard_map/while/body/eval_jaxpr/reduce_scatter | solution.py:99
  69.6 3.4 collective-permute-start
  78.0 2.0 gather_fusion
  80.1 5.4 %all_gather.12 = bf16[16,4096]{1,0:T(8,128)(2,1)S(1)} all-gather(bf16[16,1024]{1,0:T(8,128)(2,1)S(1)} %select_select_fusion.2), channel_id=1, replica_groups=mesh['groups'=2,'segment'=4,'inner'=4] {'inner'}, dimensions={1}, use_global_device_ids=true | all-gather | bytes 163840 | tf_op jit(solution)/shard_map/while/body/eval_jaxpr/all_gather | solution.py:79
  85.6 10.0 %convolution_bitcast_fusion.2 = f32[3,16,1024]{2,1,0:T(8,128)S(1)} fusion(bf16[3,4096,1024]{2,1,0:T(8,128)(2,1)} %get-tuple-element.555, bf16[16,4096]{1,0:T(8,128)(2,1)S(1)} %all_gather.12, f32[4096]{0:T(1024)} %bitcast.78, f32[16]{0:T(128)S(1)} %add_rsqrt_fusion.3), kind=kOutput, calls=%fused_computation.11.clone.1 | convolution fusion | flops 402915328 | bytes 25509952 | tf_op jit(solution)/shard_map/while/body/eval_jaxpr/bd,jdc->jbc/dot_general | solution.py:81
  96.4 5.3 %fusion.43 = f32[16,4096]{1,0:T(8,128)} fusion(bf16[1024,4096]{1,0:T(8,128)(2,1)} %get-tuple-element.560, f32[16,1024]{1,0:T(8,128)S(1)} %get-tuple-element.481, f32[3,16,1024]{2,1,0:T(8,128)S(1)} %convolution_bitcast_fusion.2), kind=kOutput, calls=%fused_computation.28.clone.1 | convolution fusion | flops 134250496 | bytes 8781824 | tf_op jit(solution)/shard_map/while/body/eval_jaxpr/dot_general | solution.py:98
  105.5 15.5 %reduce-scatter.6.cloned.1.call-done = f32[16,1024]{1,0:T(8,128)} async-done(((f32[16,4096]{1,0:T(8,128)}), f32[16,1024]{1,0:T(8,128)}) %reduce-scatter.6.cloned.1.call-update) | async-done | bytes 65552 | tf_op jit(solution)/shard_map/while/body/eval_jaxpr/reduce_scatter | solution.py:99
  121.9 3.4 collective-permute-start
  130.3 2.0 gather_fusion
  132.4 5.4 %all_gather.12 = bf16[16,4096]{1,0:T(8,128)(2,1)S(1)} all-gather(bf16[16,1024]{1,0:T(8,128)(2,1)S(1)} %select_select_fusion.2), channel_id=1, replica_groups=mesh['groups'=2,'segment'=4,'inner'=4] {'inner'}, dimensions={1}, use_global_device_ids=true | all-gather | bytes 163840 | tf_op jit(solution)/shard_map/while/body/eval_jaxpr/all_gather | solution.py:79
  138.0 10.0 %convolution_bitcast_fusion.2 = f32[3,16,1024]{2,1,0:T(8,128)S(1)} fusion(bf16[3,4096,1024]{2,1,0:T(8,128)(2,1)} %get-tuple-element.555, bf16[16,4096]{1,0:T(8,128)(2,1)S(1)} %all_gather.12, f32[4096]{0:T(1024)} %bitcast.78, f32[16]{0:T(128)S(1)} %add_rsqrt_fusion.3), kind=kOutput, calls=%fused_computation.11.clone.1 | convolution fusion | flops 402915328 | bytes 25509952 | tf_op jit(solution)/shard_map/while/body/eval_jaxpr/bd,jdc->jbc/dot_general | solution.py:81
  148.7 5.3 %fusion.43 = f32[16,4096]{1,0:T(8,128)} fusion(bf16[1024,4096]{1,0:T(8,128)(2,1)} %get-tuple-element.560, f32[16,1024]{1,0:T(8,128)S(1)} %get-tuple-element.481, f32[3,16,1024]{2,1,0:T(8,128)S(1)} %convolution_bitcast_fusion.2), kind=kOutput, calls=%fused_computation.28.clone.1 | convolution fusion | flops 134250496 | bytes 8781824 | tf_op jit(solution)/shard_map/while/body/eval_jaxpr/dot_general | solution.py:98
  157.8 15.5 %reduce-scatter.6.cloned.1.call-done = f32[16,1024]{1,0:T(8,128)} async-done(((f32[16,4096]{1,0:T(8,128)}), f32[16,1024]{1,0:T(8,128)}) %reduce-scatter.6.cloned.1.call-update) | async-done | bytes 65552 | tf_op jit(solution)/shard_map/while/body/eval_jaxpr/reduce_scatter | solution.py:99
  174.3 3.4 collective-permute-start
  182.6 2.0 gather_fusion
  184.7 5.4 %all_gather.12 = bf16[16,4096]{1,0:T(8,128)(2,1)S(1)} all-gather(bf16[16,1024]{1,0:T(8,128)(2,1)S(1)} %select_select_fusion.2), channel_id=1, replica_groups=mesh['groups'=2,'segment'=4,'inner'=4] {'inner'}, dimensions={1}, use_global_device_ids=true | all-gather | bytes 163840 | tf_op jit(solution)/shard_map/while/body/eval_jaxpr/all_gather | solution.py:79
  190.3 10.0 %convolution_bitcast_fusion.2 = f32[3,16,1024]{2,1,0:T(8,128)S(1)} fusion(bf16[3,4096,1024]{2,1,0:T(8,128)(2,1)} %get-tuple-element.555, bf16[16,4096]{1,0:T(8,128)(2,1)S(1)} %all_gather.12, f32[4096]{0:T(1024)} %bitcast.78, f32[16]{0:T(128)S(1)} %add_rsqrt_fusion.3), kind=kOutput, calls=%fused_computation.11.clone.1 | convolution fusion | flops 402915328 | bytes 25509952 | tf_op jit(solution)/shard_map/while/body/eval_jaxpr/bd,jdc->jbc/dot_general | solution.py:81
  201.0 5.3 %fusion.43 = f32[16,4096]{1,0:T(8,128)} fusion(bf16[1024,4096]{1,0:T(8,128)(2,1)} %get-tuple-element.560, f32[16,1024]{1,0:T(8,128)S(1)} %get-tuple-element.481, f32[3,16,1024]{2,1,0:T(8,128)S(1)} %convolution_bitcast_fusion.2), kind=kOutput, calls=%fused_computation.28.clone.1 | convolution fusion | flops 134250496 | bytes 8781824 | tf_op jit(solution)/shard_map/while/body/eval_jaxpr/dot_general | solution.py:98
  210.2 15.5 %reduce-scatter.6.cloned.1.call-done = f32[16,1024]{1,0:T(8,128)} async-done(((f32[16,4096]{1,0:T(8,128)}), f32[16,1024]{1,0:T(8,128)}) %reduce-scatter.6.cloned.1.call-update) | async-done | bytes 65552 | tf_op jit(solution)/shard_map/while/body/eval_jaxpr/reduce_scatter | solution.py:99
  226.6 3.4 collective-permute-start
  235.0 2.0 gather_fusion
  237.0 5.4 %all_gather.12 = bf16[16,4096]{1,0:T(8,128)(2,1)S(1)} all-gather(bf16[16,1024]{1,0:T(8,128)(2,1)S(1)} %select_select_fusion.2), channel_id=1, replica_groups=mesh['groups'=2,'segment'=4,'inner'=4] {'inner'}, dimensions={1}, use_global_device_ids=true | all-gather | bytes 163840 | tf_op jit(solution)/shard_map/while/body/eval_jaxpr/all_gather | solution.py:79
  242.6 10.0 %convolution_bitcast_fusion.2 = f32[3,16,1024]{2,1,0:T(8,128)S(1)} fusion(bf16[3,4096,1024]{2,1,0:T(8,128)(2,1)} %get-tuple-element.555, bf16[16,4096]{1,0:T(8,128)(2,1)S(1)} %all_gather.12, f32[4096]{0:T(1024)} %bitcast.78, f32[16]{0:T(128)S(1)} %add_rsqrt_fusion.3), kind=kOutput, calls=%fused_computation.11.clone.1 | convolution fusion | flops 402915328 | bytes 25509952 | tf_op jit(solution)/shard_map/while/body/eval_jaxpr/bd,jdc->jbc/dot_general | solution.py:81
  253.3 5.3 %fusion.43 = f32[16,4096]{1,0:T(8,128)} fusion(bf16[1024,4096]{1,0:T(8,128)(2,1)} %get-tuple-element.560, f32[16,1024]{1,0:T(8,128)S(1)} %get-tuple-element.481, f32[3,16,1024]{2,1,0:T(8,128)S(1)} %convolution_bitcast_fusion.2), kind=kOutput, calls=%fused_computation.28.clone.1 | convolution fusion | flops 134250496 | bytes 8781824 | tf_op jit(solution)/shard_map/while/body/eval_jaxpr/dot_general | solution.py:98
  262.5 15.5 %reduce-scatter.6.cloned.1.call-done = f32[16,1024]{1,0:T(8,128)} async-done(((f32[16,4096]{1,0:T(8,128)}), f32[16,1024]{1,0:T(8,128)}) %reduce-scatter.6.cloned.1.call-update) | async-done | bytes 65552 | tf_op jit(solution)/shard_map/while/body/eval_jaxpr/reduce_scatter | solution.py:99
  278.9 3.4 collective-permute-start
  287.3 2.0 gather_fusion
  289.4 5.4 %all_gather.12 = bf16[16,4096]{1,0:T(8,128)(2,1)S(1)} all-gather(bf16[16,1024]{1,0:T(8,128)(2,1)S(1)} %select_select_fusion.2), channel_id=1, replica_groups=mesh['groups'=2,'segment'=4,'inner'=4] {'inner'}, dimensions={1}, use_global_device_ids=true | all-gather | bytes 163840 | tf_op jit(solution)/shard_map/while/body/eval_jaxpr/all_gather | solution.py:79
  294.9 10.0 %convolution_bitcast_fusion.2 = f32[3,16,1024]{2,1,0:T(8,128)S(1)} fusion(bf16[3,4096,1024]{2,1,0:T(8,128)(2,1)} %get-tuple-element.555, bf16[16,4096]{1,0:T(8,128)(2,1)S(1)} %all_gather.12, f32[4096]{0:T(1024)} %bitcast.78, f32[16]{0:T(128)S(1)} %add_rsqrt_fusion.3), kind=kOutput, calls=%fused_computation.11.clone.1 | convolution fusion | flops 402915328 | bytes 25509952 | tf_op jit(solution)/shard_map/while/body/eval_jaxpr/bd,jdc->jbc/dot_general | solution.py:81
  305.7 5.3 %fusion.43 = f32[16,4096]{1,0:T(8,128)} fusion(bf16[1024,4096]{1,0:T(8,128)(2,1)} %get-tuple-element.560, f32[16,1024]{1,0:T(8,128)S(1)} %get-tuple-element.481, f32[3,16,1024]{2,1,0:T(8,128)S(1)} %convolution_bitcast_fusion.2), kind=kOutput, calls=%fused_computation.28.clone.1 | convolution fusion | flops 134250496 | bytes 8781824 | tf_op jit(solution)/shard_map/while/body/eval_jaxpr/dot_general | solution.py:98
  314.8 15.5 %reduce-scatter.6.cloned.1.call-done = f32[16,1024]{1,0:T(8,128)} async-done(((f32[16,4096]{1,0:T(8,128)}), f32[16,1024]{1,0:T(8,128)}) %reduce-scatter.6.cloned.1.call-update) | async-done | bytes 65552 | tf_op jit(solution)/shard_map/while/body/eval_jaxpr/reduce_scatter | solution.py:99
  331.2 3.4 collective-permute-start
  341.7 5.4 %all_gather.12 = bf16[16,4096]{1,0:T(8,128)(2,1)S(1)} all-gather(bf16[16,1024]{1,0:T(8,128)(2,1)S(1)} %select_select_fusion.2), channel_id=1, replica_groups=mesh['groups'=2,'segment'=4,'inner'=4] {'inner'}, dimensions={1}, use_global_device_ids=true | all-gather | bytes 163840 | tf_op jit(solution)/shard_map/while/body/eval_jaxpr/all_gather | solution.py:79
  347.2 10.0 %convolution_bitcast_fusion.2 = f32[3,16,1024]{2,1,0:T(8,128)S(1)} fusion(bf16[3,4096,1024]{2,1,0:T(8,128)(2,1)} %get-tuple-element.555, bf16[16,4096]{1,0:T(8,128)(2,1)S(1)} %all_gather.12, f32[4096]{0:T(1024)} %bitcast.78, f32[16]{0:T(128)S(1)} %add_rsqrt_fusion.3), kind=kOutput, calls=%fused_computation.11.clone.1 | convolution fusion | flops 402915328 | bytes 25509952 | tf_op jit(solution)/shard_map/while/body/eval_jaxpr/bd,jdc->jbc/dot_general | solution.py:81
  358.0 5.3 %fusion.43 = f32[16,4096]{1,0:T(8,128)} fusion(bf16[1024,4096]{1,0:T(8,128)(2,1)} %get-tuple-element.560, f32[16,1024]{1,0:T(8,128)S(1)} %get-tuple-element.481, f32[3,16,1024]{2,1,0:T(8,128)S(1)} %convolution_bitcast_fusion.2), kind=kOutput, calls=%fused_computation.28.clone.1 | convolution fusion | flops 134250496 | bytes 8781824 | tf_op jit(solution)/shard_map/while/body/eval_jaxpr/dot_general | solution.py:98
  367.1 15.5 %reduce-scatter.6.cloned.1.call-done = f32[16,1024]{1,0:T(8,128)} async-done(((f32[16,4096]{1,0:T(8,128)}), f32[16,1024]{1,0:T(8,128)}) %reduce-scatter.6.cloned.1.call-update) | async-done | bytes 65552 | tf_op jit(solution)/shard_map/while/body/eval_jaxpr/reduce_scatter | solution.py:99
  383.5 6.5 %all_gather.9 = bf16[2,32,4096]{2,1,0:T(8,128)(2,1)S(1)} all-gather(bf16[2,32,1024]{2,1,0:T(8,128)(2,1)S(1)} %get-tuple-element.257), channel_id=1, replica_groups=mesh['groups'=2,'segment'=4,'inner'=4] {'inner'}, dimensions={2}, use_global_device_ids=true | all-gather | bytes 655360 | tf_op jit(solution)/shard_map/all_gather | solution.py:119
  391.3 2.6 copy.27
  393.8 6.7 %all-reduce.1 = (f32[2,32]{1,0:T(2,128)S(1)}, f32[2,32]{1,0:T(2,128)S(1)}) all-reduce(f32[2,32]{1,0:T(2,128)S(1)} %get-tuple-element.321, f32[2,32]{1,0:T(2,128)S(1)} %get-tuple-element.320), channel_id=1, replica_groups=mesh['groups'=2,'segment'=4,'inner'=4] {'inner'}, use_global_device_ids=true, to_apply=%region_11.12 | all-reduce | flops 128 | bytes 1024 | tf_op jit(solution)/shard_map/psum | solution.py:129
  400.6 11.7 %all-reduce = f32[2,32]{1,0:T(2,128)S(1)} all-reduce(f32[2,32]{1,0:T(2,128)S(1)} %subtract_select_fusion), channel_id=4, replica_groups=mesh['groups'=2,'segment'=4,'inner'=4] {'segment'}, use_global_device_ids=true, to_apply=%region_14.15.clone | all-reduce | flops 64 | bytes 512
  (211 shorter events, 80.9 us)
Async XLA Ops:
  8.0 382.3 %copy-start = (bf16[4096,128]{1,0:T(8,128)(2,1)S(1)}, bf16[4096,128]{1,0:T(8,128)(2,1)}, u32[]{:S(2)}) copy-start(bf16[4096,128]{1,0:T(8,128)(2,1)} %param.27) | copy-start | bytes 3145732
  14.5 375.8 %copy-start.3 = (f32[4096]{0:T(1024)S(1)}, f32[4096]{0:T(1024)}, u32[]{:S(2)}) copy-start(f32[4096]{0:T(1024)} %param.26) | copy-start | bytes 49156
  14.5 397.8 %copy-start.4 = (u32[32]{0:T(128)S(1)}, u32[32]{0:T(128)}, u32[]{:S(2)}) copy-start(u32[32]{0:T(128)} %constant.157) | copy-start | bytes 388
  14.5 54.2 %reduce-scatter.6.cloned.1.call-start = ((), (), s32[]{:S(2)}) async-start(), calls=%async_computation.3 | async-start | bytes 327680 | tf_op jit(solution)/shard_map/while/body/eval_jaxpr/reduce_scatter | solution.py:99
  14.6 11.9 %collective-permute-start = (bf16[16,1024]{1,0:T(8,128)(2,1)S(1)}, bf16[16,1024]{1,0:T(8,128)(2,1)S(1)}, u32[]{:S(2)}, u32[]{:S(2)}) collective-permute-start(bf16[16,1024]{1,0:T(8,128)(2,1)S(1)} %broadcast_select_fusion.3), channel_id=1, source_target_pairs={{0,4},{4,8},{8,12},{1,5},{5,9},{9,13},{2,6},{6,10},{10,14},{3,7},{... | collective-permute-start | bytes 98312 | tf_op jit(solution)/shard_map/while/body/eval_jaxpr/ppermute | solution.py:12
  26.5 15.7 %copy-start.1 = (f32[1,8,1024]{2,1,0:T(8,128)S(1)}, f32[1,8,1024]{2,1,0:T(8,128)}, u32[]{:S(2)}) copy-start(f32[1,8,1024]{2,1,0:T(8,128)} %get-tuple-element.557) | copy-start | bytes 98308 | tf_op jit(solution)/shard_map/while
  26.5 15.6 %copy-start.2 = (f32[8,1024]{1,0:T(8,128)S(1)}, f32[8,1024]{1,0:T(8,128)}, u32[]{:S(2)}) copy-start(f32[8,1024]{1,0:T(8,128)} %get-tuple-element.558) | copy-start | bytes 98308 | tf_op jit(solution)/shard_map/while
  69.5 51.5 %reduce-scatter.6.cloned.1.call-start = ((), (), s32[]{:S(2)}) async-start(), calls=%async_computation.3 | async-start | bytes 327680 | tf_op jit(solution)/shard_map/while/body/eval_jaxpr/reduce_scatter | solution.py:99
  69.6 10.4 %collective-permute-start = (bf16[16,1024]{1,0:T(8,128)(2,1)S(1)}, bf16[16,1024]{1,0:T(8,128)(2,1)S(1)}, u32[]{:S(2)}, u32[]{:S(2)}) collective-permute-start(bf16[16,1024]{1,0:T(8,128)(2,1)S(1)} %broadcast_select_fusion.3), channel_id=1, source_target_pairs={{0,4},{4,8},{8,12},{1,5},{5,9},{9,13},{2,6},{6,10},{10,14},{3,7},{... | collective-permute-start | bytes 98312 | tf_op jit(solution)/shard_map/while/body/eval_jaxpr/ppermute | solution.py:12
  80.0 15.7 %copy-start.1 = (f32[1,8,1024]{2,1,0:T(8,128)S(1)}, f32[1,8,1024]{2,1,0:T(8,128)}, u32[]{:S(2)}) copy-start(f32[1,8,1024]{2,1,0:T(8,128)} %get-tuple-element.557) | copy-start | bytes 98308 | tf_op jit(solution)/shard_map/while
  80.0 15.6 %copy-start.2 = (f32[8,1024]{1,0:T(8,128)S(1)}, f32[8,1024]{1,0:T(8,128)}, u32[]{:S(2)}) copy-start(f32[8,1024]{1,0:T(8,128)} %get-tuple-element.558) | copy-start | bytes 98308 | tf_op jit(solution)/shard_map/while
  121.9 51.5 %reduce-scatter.6.cloned.1.call-start = ((), (), s32[]{:S(2)}) async-start(), calls=%async_computation.3 | async-start | bytes 327680 | tf_op jit(solution)/shard_map/while/body/eval_jaxpr/reduce_scatter | solution.py:99
  121.9 10.4 %collective-permute-start = (bf16[16,1024]{1,0:T(8,128)(2,1)S(1)}, bf16[16,1024]{1,0:T(8,128)(2,1)S(1)}, u32[]{:S(2)}, u32[]{:S(2)}) collective-permute-start(bf16[16,1024]{1,0:T(8,128)(2,1)S(1)} %broadcast_select_fusion.3), channel_id=1, source_target_pairs={{0,4},{4,8},{8,12},{1,5},{5,9},{9,13},{2,6},{6,10},{10,14},{3,7},{... | collective-permute-start | bytes 98312 | tf_op jit(solution)/shard_map/while/body/eval_jaxpr/ppermute | solution.py:12
  132.3 15.7 %copy-start.1 = (f32[1,8,1024]{2,1,0:T(8,128)S(1)}, f32[1,8,1024]{2,1,0:T(8,128)}, u32[]{:S(2)}) copy-start(f32[1,8,1024]{2,1,0:T(8,128)} %get-tuple-element.557) | copy-start | bytes 98308 | tf_op jit(solution)/shard_map/while
  132.3 15.6 %copy-start.2 = (f32[8,1024]{1,0:T(8,128)S(1)}, f32[8,1024]{1,0:T(8,128)}, u32[]{:S(2)}) copy-start(f32[8,1024]{1,0:T(8,128)} %get-tuple-element.558) | copy-start | bytes 98308 | tf_op jit(solution)/shard_map/while
  174.2 51.4 %reduce-scatter.6.cloned.1.call-start = ((), (), s32[]{:S(2)}) async-start(), calls=%async_computation.3 | async-start | bytes 327680 | tf_op jit(solution)/shard_map/while/body/eval_jaxpr/reduce_scatter | solution.py:99
  174.3 10.4 %collective-permute-start = (bf16[16,1024]{1,0:T(8,128)(2,1)S(1)}, bf16[16,1024]{1,0:T(8,128)(2,1)S(1)}, u32[]{:S(2)}, u32[]{:S(2)}) collective-permute-start(bf16[16,1024]{1,0:T(8,128)(2,1)S(1)} %broadcast_select_fusion.3), channel_id=1, source_target_pairs={{0,4},{4,8},{8,12},{1,5},{5,9},{9,13},{2,6},{6,10},{10,14},{3,7},{... | collective-permute-start | bytes 98312 | tf_op jit(solution)/shard_map/while/body/eval_jaxpr/ppermute | solution.py:12
  184.6 15.7 %copy-start.1 = (f32[1,8,1024]{2,1,0:T(8,128)S(1)}, f32[1,8,1024]{2,1,0:T(8,128)}, u32[]{:S(2)}) copy-start(f32[1,8,1024]{2,1,0:T(8,128)} %get-tuple-element.557) | copy-start | bytes 98308 | tf_op jit(solution)/shard_map/while
  184.6 15.6 %copy-start.2 = (f32[8,1024]{1,0:T(8,128)S(1)}, f32[8,1024]{1,0:T(8,128)}, u32[]{:S(2)}) copy-start(f32[8,1024]{1,0:T(8,128)} %get-tuple-element.558) | copy-start | bytes 98308 | tf_op jit(solution)/shard_map/while
  226.5 51.4 %reduce-scatter.6.cloned.1.call-start = ((), (), s32[]{:S(2)}) async-start(), calls=%async_computation.3 | async-start | bytes 327680 | tf_op jit(solution)/shard_map/while/body/eval_jaxpr/reduce_scatter | solution.py:99
  226.6 10.4 %collective-permute-start = (bf16[16,1024]{1,0:T(8,128)(2,1)S(1)}, bf16[16,1024]{1,0:T(8,128)(2,1)S(1)}, u32[]{:S(2)}, u32[]{:S(2)}) collective-permute-start(bf16[16,1024]{1,0:T(8,128)(2,1)S(1)} %broadcast_select_fusion.3), channel_id=1, source_target_pairs={{0,4},{4,8},{8,12},{1,5},{5,9},{9,13},{2,6},{6,10},{10,14},{3,7},{... | collective-permute-start | bytes 98312 | tf_op jit(solution)/shard_map/while/body/eval_jaxpr/ppermute | solution.py:12
  236.9 15.7 %copy-start.1 = (f32[1,8,1024]{2,1,0:T(8,128)S(1)}, f32[1,8,1024]{2,1,0:T(8,128)}, u32[]{:S(2)}) copy-start(f32[1,8,1024]{2,1,0:T(8,128)} %get-tuple-element.557) | copy-start | bytes 98308 | tf_op jit(solution)/shard_map/while
  236.9 15.6 %copy-start.2 = (f32[8,1024]{1,0:T(8,128)S(1)}, f32[8,1024]{1,0:T(8,128)}, u32[]{:S(2)}) copy-start(f32[8,1024]{1,0:T(8,128)} %get-tuple-element.558) | copy-start | bytes 98308 | tf_op jit(solution)/shard_map/while
  278.8 51.4 %reduce-scatter.6.cloned.1.call-start = ((), (), s32[]{:S(2)}) async-start(), calls=%async_computation.3 | async-start | bytes 327680 | tf_op jit(solution)/shard_map/while/body/eval_jaxpr/reduce_scatter | solution.py:99
  278.9 10.4 %collective-permute-start = (bf16[16,1024]{1,0:T(8,128)(2,1)S(1)}, bf16[16,1024]{1,0:T(8,128)(2,1)S(1)}, u32[]{:S(2)}, u32[]{:S(2)}) collective-permute-start(bf16[16,1024]{1,0:T(8,128)(2,1)S(1)} %broadcast_select_fusion.3), channel_id=1, source_target_pairs={{0,4},{4,8},{8,12},{1,5},{5,9},{9,13},{2,6},{6,10},{10,14},{3,7},{... | collective-permute-start | bytes 98312 | tf_op jit(solution)/shard_map/while/body/eval_jaxpr/ppermute | solution.py:12
  289.2 15.7 %copy-start.1 = (f32[1,8,1024]{2,1,0:T(8,128)S(1)}, f32[1,8,1024]{2,1,0:T(8,128)}, u32[]{:S(2)}) copy-start(f32[1,8,1024]{2,1,0:T(8,128)} %get-tuple-element.557) | copy-start | bytes 98308 | tf_op jit(solution)/shard_map/while
  289.3 15.6 %copy-start.2 = (f32[8,1024]{1,0:T(8,128)S(1)}, f32[8,1024]{1,0:T(8,128)}, u32[]{:S(2)}) copy-start(f32[8,1024]{1,0:T(8,128)} %get-tuple-element.558) | copy-start | bytes 98308 | tf_op jit(solution)/shard_map/while
  331.2 51.4 %reduce-scatter.6.cloned.1.call-start = ((), (), s32[]{:S(2)}) async-start(), calls=%async_computation.3 | async-start | bytes 327680 | tf_op jit(solution)/shard_map/while/body/eval_jaxpr/reduce_scatter | solution.py:99
  331.2 10.4 %collective-permute-start = (bf16[16,1024]{1,0:T(8,128)(2,1)S(1)}, bf16[16,1024]{1,0:T(8,128)(2,1)S(1)}, u32[]{:S(2)}, u32[]{:S(2)}) collective-permute-start(bf16[16,1024]{1,0:T(8,128)(2,1)S(1)} %broadcast_select_fusion.3), channel_id=1, source_target_pairs={{0,4},{4,8},{8,12},{1,5},{5,9},{9,13},{2,6},{6,10},{10,14},{3,7},{... | collective-permute-start | bytes 98312 | tf_op jit(solution)/shard_map/while/body/eval_jaxpr/ppermute | solution.py:12
  341.6 15.7 %copy-start.1 = (f32[1,8,1024]{2,1,0:T(8,128)S(1)}, f32[1,8,1024]{2,1,0:T(8,128)}, u32[]{:S(2)}) copy-start(f32[1,8,1024]{2,1,0:T(8,128)} %get-tuple-element.557) | copy-start | bytes 98308 | tf_op jit(solution)/shard_map/while
  341.6 15.6 %copy-start.2 = (f32[8,1024]{1,0:T(8,128)S(1)}, f32[8,1024]{1,0:T(8,128)}, u32[]{:S(2)}) copy-start(f32[8,1024]{1,0:T(8,128)} %get-tuple-element.558) | copy-start | bytes 98308 | tf_op jit(solution)/shard_map/while
  383.5 30.7 %reduce-scatter.4.cloned.1.call-start = ((), (), s32[]{:S(2)}) async-start(), calls=%async_computation.2 | async-start | bytes 40960 | tf_op jit(solution)/shard_map/reduce_scatter | solution.py:134
Sparse Core Ops, SparseCore 0:
  48.3 20.2 reduce-scatter.5
  101.8 19.1 reduce-scatter.5
  154.1 19.1 reduce-scatter.5
  206.5 19.1 reduce-scatter.5
  258.8 19.1 reduce-scatter.5
  311.1 19.1 reduce-scatter.5
  363.4 19.1 reduce-scatter.5
Sparse Core Ops, SparseCore 1:
  391.4 19.8 reduce-scatter.3
where the time goes:
time: 425 us; the launch traced here: 422 us
  waiting for transfers between devices  110 us (26%)
  matrix products  108 us (25%)
  blocking collectives  62.8 us (15%)
  other arithmetic  48.1 us (11%)
  local copies, waits for them, and re-layouts  45.5 us (11%)
  starting transfers between devices  25.7 us (6%)
  between operations  16.2 us (4%)
  loops' own time  6.16 us (1%)
    reduce_scatter x7, waiting for transfers between devices, advance(): lax.psum_scatter(partial_sum, 'inner', scatter_dimension=1, tiled=True)  109 us
    dot_general x7, matrix products, advance(): jnp.einsum('bd,jdc->jbc', normalized, w_in, preferred_element_type=jnp.fl...  69.7 us
    all_gather x7, blocking collectives, advance(): gathered = lax.all_gather(stream_in, 'inner', axis=1, tiled=True)  37.8 us
    dot_general x7, matrix products, advance(): partial_sum = jnp.dot(gated_rows, w_out, preferred_element_type=jnp.float32)  37.1 us
    ppermute x7, starting transfers between devices, from_behind(): return lax.ppermute(block, axis, route)  25.3 us
    gather x7, local copies, waits for them, and re-layouts, advance(): looked_up = jnp.take(embedding, token_ids, axis=0)  13.8 us
    dynamic_update_slice x7, other arithmetic, advance(): lax.dynamic_update_slice_in_dim(fir_all, jnp.where(is_valid, fir_next, fi...  13.4 us
    dynamic_update_slice x7, other arithmetic, advance(): lax.dynamic_update_slice_in_dim(modal_all, jnp.where(is_valid, modal_next...  13.2 us
  transfers between devices with their start and end apart: 15, of which 7 were waited for; matrix products, arithmetic and copies ran while one was open for 18% of the time, Pallas kernels for 0%

commit v1 on v0

--- a/solution.py
+++ b/solution.py
@@ -2,8 +2,24 @@
 import jax.numpy as jnp
 from jax import lax
 from jax.sharding import PartitionSpec as P
+from jax.lax import axis_index, axis_size, ppermute
 
 MICRO = 2
+
+
+def strips_all_attach(chunk):
+    axis_key = "inner"
+    n_dev_all = axis_size(axis_key)
+    r_now = sorted(((q, (q + 1) % n_dev_all) for q in range(n_dev_all)))
+    next_value = chunk
+    cards = [next_value]
+    for src_i in range(1, n_dev_all):
+        next_value = ppermute(next_value, axis_name=axis_key, perm=r_now)
+        cards.insert(0, next_value)
+    before = jnp.concatenate(cards, 1)
+    block_now = axis_index(axis_key)
+    raw_out = block_now + 1
+    return jnp.roll(before, shift=raw_out * chunk.shape[1], axis=1)
 
 
 def from_behind(block, axis, distance):
@@ -76,7 +92,7 @@
         token_ids = lax.dynamic_slice(tokens, (step_index, row_start), (1, row_count))[0]
         looked_up = jnp.take(embedding, token_ids, axis=0)
         stream_in = jnp.where(segment_index == 0, looked_up, incoming)
-        gathered = lax.all_gather(stream_in, "inner", axis=1, tiled=True)
+        gathered = strips_all_attach(stream_in)
         normalized = normed(gathered.astype(jnp.float32), gain_local).astype(jnp.bfloat16)
         projected = jnp.einsum("bd,jdc->jbc", normalized, w_in, preferred_element_type=jnp.float32)
         product = projected[1] * projected[2]

time: 425 us -> 442 us (1.040)
  waiting for transfers between devices: 110 us -> 164 us
  blocking collectives: 62.8 us -> 25 us
    ppermute x0 -> x21, waiting for transfers between devices: none -> 54.8 us  [strips_all_attach(): next_value = ppermute(next_value, axis_name=axis_key, perm=r_now)]
    all_gather x7 -> x0, blocking collectives: 37.8 us -> none  [advance(): gathered = lax.all_gather(stream_in, 'inner', axis=1, tiled=True)]
  transfers between devices with their start and end apart: 15 -> 36, of which waited for: 7 -> 28; matrix products, arithmetic and copies ran while one was open for 18% -> 17% of each run, Pallas kernels for 0% -> 0%
where the time goes in v1:
time: 442 us; the launch traced here: 439 us
  waiting for transfers between devices  164 us (37%)
  matrix products  108 us (24%)
  other arithmetic  48.1 us (11%)
  local copies, waits for them, and re-layouts  45.6 us (10%)
  starting transfers between devices  25.7 us (6%)
  blocking collectives  25 us (6%)
  between operations  16.2 us (4%)
  loops' own time  6.65 us (2%)
    reduce_scatter x7, waiting for transfers between devices, advance(): lax.psum_scatter(partial_sum, 'inner', scatter_dimension=1, tiled=True)  109 us
    dot_general x7, matrix products, advance(): jnp.einsum('bd,jdc->jbc', normalized, w_in, preferred_element_type=jnp.fl...  69.7 us
    ppermute x21, waiting for transfers between devices, strips_all_attach(): next_value = ppermute(next_value, axis_name=axis_key, perm=r_now)  54.8 us
    dot_general x7, matrix products, advance(): partial_sum = jnp.dot(gated_rows, w_out, preferred_element_type=jnp.float32)  37.1 us
    ppermute x7, starting transfers between devices, from_behind(): return lax.ppermute(block, axis, route)  25.3 us
    gather x7, local copies, waits for them, and re-layouts, advance(): looked_up = jnp.take(embedding, token_ids, axis=0)  13.8 us
    dynamic_update_slice x7, other arithmetic, advance(): lax.dynamic_update_slice_in_dim(fir_all, jnp.where(is_valid, fir_next, fi...  13.4 us
    dynamic_update_slice x7, other arithmetic, advance(): lax.dynamic_update_slice_in_dim(modal_all, jnp.where(is_valid, modal_next...  13.2 us
  transfers between devices with their start and end apart: 36, of which 28 were waited for; matrix products, arithmetic and copies ran while one was open for 17% of the time, Pallas kernels for 0%

profile of v1, /device:TPU:0, one launch (start us, length us, event | category | flops | bytes accessed | tf_op | source)
XLA Modules:
  0.0 439.3 jit_solution(1035222231934657969)
XLA Ops:
  8.0 2.4 copy.63
  10.4 2.6 copy.26
  14.5 386.7 %while.20 = (s32[]{:T(128)}, bf16[16,1024]{1,0:T(8,128)(2,1)S(1)}, f32[32,6,1024]{2,1,0:T(8,128)}, f32[32,8,1024]{2,1,0:T(8,128)}, bf16[2,32,1024]{2,1,0:T(8,128...) while((s32[]{:T(128)}, bf16[16,1024]{1,0:T(8,128)(2,1)S(1)}, ...), condition=%wide.region_7.8_spmd.clone, body=%wide.region_0.7_spmd.clone.sunk | while | flops 538412288 | bytes 44574912 | solution.py:133
  14.6 5.0 %collective-permute-start = (bf16[16,1024]{1,0:T(8,128)(2,1)S(1)}, bf16[16,1024]{1,0:T(8,128)(2,1)S(1)}, u32[]{:S(2)}, u32[]{:S(2)}) collective-permute-start(bf16[16,1024]{1,0:T(8,128)(2,1)S(1)} %broadcast_select_fusion.3), channel_id=1, source_target_pairs={{0,4},{4,8},{8,12},{1,5},{5,9},{9,13},{2,6},{6,10},{10,14},{3,7},{... | collective-permute-start | bytes 98312 | tf_op jit(solution)/shard_map/while/body/eval_jaxpr/ppermute | solution.py:28
  24.4 3.3 collective-permute-done.1
  28.8 2.3 collective-permute-done.2
  34.7 10.0 %convolution_bitcast_fusion.2 = f32[3,16,1024]{2,1,0:T(8,128)S(1)} fusion(bf16[3,4096,1024]{2,1,0:T(8,128)(2,1)} %get-tuple-element.619, f32[4096]{0:T(1024)} %bitcast.78, f32[16]{0:T(128)S(1)} %add_rsqrt_fusion.3, bf16[16,8192]{1,0:T(8,128)(2,1)S(1)} %constant_dynamic-update-slice_fusion.23, s32[]{:T(128)S(6)} %select_n.272), kind=kOutput, calls=%fused_computation.11.clone.1 | convolution fusion | flops 402915328 | bytes 25510404 | tf_op jit(solution)/shard_map/while/body/eval_jaxpr/bd,jdc->jbc/dot_general | solution.py:97
  45.4 5.3 %fusion.45 = f32[16,4096]{1,0:T(8,128)} fusion(bf16[1024,4096]{1,0:T(8,128)(2,1)} %get-tuple-element.624, f32[16,1024]{1,0:T(8,128)S(1)} %get-tuple-element.535, f32[3,16,1024]{2,1,0:T(8,128)S(1)} %convolution_bitcast_fusion.2), kind=kOutput, calls=%fused_computation.29.clone.1 | convolution fusion | flops 134250496 | bytes 8781824 | tf_op jit(solution)/shard_map/while/body/eval_jaxpr/dot_general | solution.py:114
  54.6 16.6 %reduce-scatter.6.cloned.1.call-done = f32[16,1024]{1,0:T(8,128)} async-done(((f32[16,4096]{1,0:T(8,128)}), f32[16,1024]{1,0:T(8,128)}) %reduce-scatter.6.cloned.1.call-update) | async-done | bytes 65552 | tf_op jit(solution)/shard_map/while/body/eval_jaxpr/reduce_scatter | solution.py:115
  72.1 3.4 collective-permute-start
  80.4 3.3 collective-permute-done.1
  84.8 2.3 collective-permute-done.2
  90.7 10.0 %convolution_bitcast_fusion.2 = f32[3,16,1024]{2,1,0:T(8,128)S(1)} fusion(bf16[3,4096,1024]{2,1,0:T(8,128)(2,1)} %get-tuple-element.619, f32[4096]{0:T(1024)} %bitcast.78, f32[16]{0:T(128)S(1)} %add_rsqrt_fusion.3, bf16[16,8192]{1,0:T(8,128)(2,1)S(1)} %constant_dynamic-update-slice_fusion.23, s32[]{:T(128)S(6)} %select_n.272), kind=kOutput, calls=%fused_computation.11.clone.1 | convolution fusion | flops 402915328 | bytes 25510404 | tf_op jit(solution)/shard_map/while/body/eval_jaxpr/bd,jdc->jbc/dot_general | solution.py:97
  101.4 5.3 %fusion.45 = f32[16,4096]{1,0:T(8,128)} fusion(bf16[1024,4096]{1,0:T(8,128)(2,1)} %get-tuple-element.624, f32[16,1024]{1,0:T(8,128)S(1)} %get-tuple-element.535, f32[3,16,1024]{2,1,0:T(8,128)S(1)} %convolution_bitcast_fusion.2), kind=kOutput, calls=%fused_computation.29.clone.1 | convolution fusion | flops 134250496 | bytes 8781824 | tf_op jit(solution)/shard_map/while/body/eval_jaxpr/dot_general | solution.py:114
  110.6 15.5 %reduce-scatter.6.cloned.1.call-done = f32[16,1024]{1,0:T(8,128)} async-done(((f32[16,4096]{1,0:T(8,128)}), f32[16,1024]{1,0:T(8,128)}) %reduce-scatter.6.cloned.1.call-update) | async-done | bytes 65552 | tf_op jit(solution)/shard_map/while/body/eval_jaxpr/reduce_scatter | solution.py:115
  127.0 3.4 collective-permute-start
  135.3 3.3 collective-permute-done.1
  139.7 2.3 collective-permute-done.2
  145.5 10.0 %convolution_bitcast_fusion.2 = f32[3,16,1024]{2,1,0:T(8,128)S(1)} fusion(bf16[3,4096,1024]{2,1,0:T(8,128)(2,1)} %get-tuple-element.619, f32[4096]{0:T(1024)} %bitcast.78, f32[16]{0:T(128)S(1)} %add_rsqrt_fusion.3, bf16[16,8192]{1,0:T(8,128)(2,1)S(1)} %constant_dynamic-update-slice_fusion.23, s32[]{:T(128)S(6)} %select_n.272), kind=kOutput, calls=%fused_computation.11.clone.1 | convolution fusion | flops 402915328 | bytes 25510404 | tf_op jit(solution)/shard_map/while/body/eval_jaxpr/bd,jdc->jbc/dot_general | solution.py:97
  156.3 5.3 %fusion.45 = f32[16,4096]{1,0:T(8,128)} fusion(bf16[1024,4096]{1,0:T(8,128)(2,1)} %get-tuple-element.624, f32[16,1024]{1,0:T(8,128)S(1)} %get-tuple-element.535, f32[3,16,1024]{2,1,0:T(8,128)S(1)} %convolution_bitcast_fusion.2), kind=kOutput, calls=%fused_computation.29.clone.1 | convolution fusion | flops 134250496 | bytes 8781824 | tf_op jit(solution)/shard_map/while/body/eval_jaxpr/dot_general | solution.py:114
  165.4 15.5 %reduce-scatter.6.cloned.1.call-done = f32[16,1024]{1,0:T(8,128)} async-done(((f32[16,4096]{1,0:T(8,128)}), f32[16,1024]{1,0:T(8,128)}) %reduce-scatter.6.cloned.1.call-update) | async-done | bytes 65552 | tf_op jit(solution)/shard_map/while/body/eval_jaxpr/reduce_scatter | solution.py:115
  181.8 3.4 collective-permute-start
  190.1 3.3 collective-permute-done.1
  194.5 2.3 collective-permute-done.2
  200.4 10.0 %convolution_bitcast_fusion.2 = f32[3,16,1024]{2,1,0:T(8,128)S(1)} fusion(bf16[3,4096,1024]{2,1,0:T(8,128)(2,1)} %get-tuple-element.619, f32[4096]{0:T(1024)} %bitcast.78, f32[16]{0:T(128)S(1)} %add_rsqrt_fusion.3, bf16[16,8192]{1,0:T(8,128)(2,1)S(1)} %constant_dynamic-update-slice_fusion.23, s32[]{:T(128)S(6)} %select_n.272), kind=kOutput, calls=%fused_computation.11.clone.1 | convolution fusion | flops 402915328 | bytes 25510404 | tf_op jit(solution)/shard_map/while/body/eval_jaxpr/bd,jdc->jbc/dot_general | solution.py:97
  211.1 5.3 %fusion.45 = f32[16,4096]{1,0:T(8,128)} fusion(bf16[1024,4096]{1,0:T(8,128)(2,1)} %get-tuple-element.624, f32[16,1024]{1,0:T(8,128)S(1)} %get-tuple-element.535, f32[3,16,1024]{2,1,0:T(8,128)S(1)} %convolution_bitcast_fusion.2), kind=kOutput, calls=%fused_computation.29.clone.1 | convolution fusion | flops 134250496 | bytes 8781824 | tf_op jit(solution)/shard_map/while/body/eval_jaxpr/dot_general | solution.py:114
  220.3 15.5 %reduce-scatter.6.cloned.1.call-done = f32[16,1024]{1,0:T(8,128)} async-done(((f32[16,4096]{1,0:T(8,128)}), f32[16,1024]{1,0:T(8,128)}) %reduce-scatter.6.cloned.1.call-update) | async-done | bytes 65552 | tf_op jit(solution)/shard_map/while/body/eval_jaxpr/reduce_scatter | solution.py:115
  236.7 3.4 collective-permute-start
  245.0 3.3 collective-permute-done.1
  249.4 2.3 collective-permute-done.2
  255.3 10.0 %convolution_bitcast_fusion.2 = f32[3,16,1024]{2,1,0:T(8,128)S(1)} fusion(bf16[3,4096,1024]{2,1,0:T(8,128)(2,1)} %get-tuple-element.619, f32[4096]{0:T(1024)} %bitcast.78, f32[16]{0:T(128)S(1)} %add_rsqrt_fusion.3, bf16[16,8192]{1,0:T(8,128)(2,1)S(1)} %constant_dynamic-update-slice_fusion.23, s32[]{:T(128)S(6)} %select_n.272), kind=kOutput, calls=%fused_computation.11.clone.1 | convolution fusion | flops 402915328 | bytes 25510404 | tf_op jit(solution)/shard_map/while/body/eval_jaxpr/bd,jdc->jbc/dot_general | solution.py:97
  266.0 5.3 %fusion.45 = f32[16,4096]{1,0:T(8,128)} fusion(bf16[1024,4096]{1,0:T(8,128)(2,1)} %get-tuple-element.624, f32[16,1024]{1,0:T(8,128)S(1)} %get-tuple-element.535, f32[3,16,1024]{2,1,0:T(8,128)S(1)} %convolution_bitcast_fusion.2), kind=kOutput, calls=%fused_computation.29.clone.1 | convolution fusion | flops 134250496 | bytes 8781824 | tf_op jit(solution)/shard_map/while/body/eval_jaxpr/dot_general | solution.py:114
  275.2 15.5 %reduce-scatter.6.cloned.1.call-done = f32[16,1024]{1,0:T(8,128)} async-done(((f32[16,4096]{1,0:T(8,128)}), f32[16,1024]{1,0:T(8,128)}) %reduce-scatter.6.cloned.1.call-update) | async-done | bytes 65552 | tf_op jit(solution)/shard_map/while/body/eval_jaxpr/reduce_scatter | solution.py:115
  291.6 3.4 collective-permute-start
  299.8 3.3 collective-permute-done.1
  304.2 2.3 collective-permute-done.2
  310.1 10.0 %convolution_bitcast_fusion.2 = f32[3,16,1024]{2,1,0:T(8,128)S(1)} fusion(bf16[3,4096,1024]{2,1,0:T(8,128)(2,1)} %get-tuple-element.619, f32[4096]{0:T(1024)} %bitcast.78, f32[16]{0:T(128)S(1)} %add_rsqrt_fusion.3, bf16[16,8192]{1,0:T(8,128)(2,1)S(1)} %constant_dynamic-update-slice_fusion.23, s32[]{:T(128)S(6)} %select_n.272), kind=kOutput, calls=%fused_computation.11.clone.1 | convolution fusion | flops 402915328 | bytes 25510404 | tf_op jit(solution)/shard_map/while/body/eval_jaxpr/bd,jdc->jbc/dot_general | solution.py:97
  320.9 5.3 %fusion.45 = f32[16,4096]{1,0:T(8,128)} fusion(bf16[1024,4096]{1,0:T(8,128)(2,1)} %get-tuple-element.624, f32[16,1024]{1,0:T(8,128)S(1)} %get-tuple-element.535, f32[3,16,1024]{2,1,0:T(8,128)S(1)} %convolution_bitcast_fusion.2), kind=kOutput, calls=%fused_computation.29.clone.1 | convolution fusion | flops 134250496 | bytes 8781824 | tf_op jit(solution)/shard_map/while/body/eval_jaxpr/dot_general | solution.py:114
  330.0 15.5 %reduce-scatter.6.cloned.1.call-done = f32[16,1024]{1,0:T(8,128)} async-done(((f32[16,4096]{1,0:T(8,128)}), f32[16,1024]{1,0:T(8,128)}) %reduce-scatter.6.cloned.1.call-update) | async-done | bytes 65552 | tf_op jit(solution)/shard_map/while/body/eval_jaxpr/reduce_scatter | solution.py:115
  346.4 3.4 collective-permute-start
  354.7 3.3 collective-permute-done.1
  365.0 10.0 %convolution_bitcast_fusion.2 = f32[3,16,1024]{2,1,0:T(8,128)S(1)} fusion(bf16[3,4096,1024]{2,1,0:T(8,128)(2,1)} %get-tuple-element.619, f32[4096]{0:T(1024)} %bitcast.78, f32[16]{0:T(128)S(1)} %add_rsqrt_fusion.3, bf16[16,8192]{1,0:T(8,128)(2,1)S(1)} %constant_dynamic-update-slice_fusion.23, s32[]{:T(128)S(6)} %select_n.272), kind=kOutput, calls=%fused_computation.11.clone.1 | convolution fusion | flops 402915328 | bytes 25510404 | tf_op jit(solution)/shard_map/while/body/eval_jaxpr/bd,jdc->jbc/dot_general | solution.py:97
  375.7 5.3 %fusion.45 = f32[16,4096]{1,0:T(8,128)} fusion(bf16[1024,4096]{1,0:T(8,128)(2,1)} %get-tuple-element.624, f32[16,1024]{1,0:T(8,128)S(1)} %get-tuple-element.535, f32[3,16,1024]{2,1,0:T(8,128)S(1)} %convolution_bitcast_fusion.2), kind=kOutput, calls=%fused_computation.29.clone.1 | convolution fusion | flops 134250496 | bytes 8781824 | tf_op jit(solution)/shard_map/while/body/eval_jaxpr/dot_general | solution.py:114
  384.9 15.5 %reduce-scatter.6.cloned.1.call-done = f32[16,1024]{1,0:T(8,128)} async-done(((f32[16,4096]{1,0:T(8,128)}), f32[16,1024]{1,0:T(8,128)}) %reduce-scatter.6.cloned.1.call-update) | async-done | bytes 65552 | tf_op jit(solution)/shard_map/while/body/eval_jaxpr/reduce_scatter | solution.py:115
  401.2 6.6 %all_gather.3 = bf16[2,32,4096]{2,1,0:T(8,128)(2,1)S(1)} all-gather(bf16[2,32,1024]{2,1,0:T(8,128)(2,1)S(1)} %get-tuple-element.311), channel_id=1, replica_groups=mesh['groups'=2,'segment'=4,'inner'=4] {'inner'}, dimensions={2}, use_global_device_ids=true | all-gather | bytes 655360 | tf_op jit(solution)/shard_map/all_gather | solution.py:135
  409.0 2.6 copy.27
  411.6 6.7 %all-reduce.1 = (f32[2,32]{1,0:T(2,128)S(1)}, f32[2,32]{1,0:T(2,128)S(1)}) all-reduce(f32[2,32]{1,0:T(2,128)S(1)} %get-tuple-element.375, f32[2,32]{1,0:T(2,128)S(1)} %get-tuple-element.374), channel_id=1, replica_groups=mesh['groups'=2,'segment'=4,'inner'=4] {'inner'}, use_global_device_ids=true, to_apply=%region_11.12 | all-reduce | flops 128 | bytes 1024 | tf_op jit(solution)/shard_map/psum | solution.py:145
  418.3 11.7 %all-reduce = f32[2,32]{1,0:T(2,128)S(1)} all-reduce(f32[2,32]{1,0:T(2,128)S(1)} %subtract_select_fusion), channel_id=4, replica_groups=mesh['groups'=2,'segment'=4,'inner'=4] {'segment'}, use_global_device_ids=true, to_apply=%region_14.15.clone | all-reduce | flops 64 | bytes 512
  (302 shorter events, 110.8 us)
Async XLA Ops:
  8.0 400.0 %copy-start = (bf16[4096,128]{1,0:T(8,128)(2,1)S(1)}, bf16[4096,128]{1,0:T(8,128)(2,1)}, u32[]{:S(2)}) copy-start(bf16[4096,128]{1,0:T(8,128)(2,1)} %param.27) | copy-start | bytes 3145732
  14.5 393.5 %copy-start.3 = (f32[4096]{0:T(1024)S(1)}, f32[4096]{0:T(1024)}, u32[]{:S(2)}) copy-start(f32[4096]{0:T(1024)} %param.26) | copy-start | bytes 49156
  14.5 415.6 %copy-start.4 = (u32[32]{0:T(128)S(1)}, u32[32]{0:T(128)}, u32[]{:S(2)}) copy-start(u32[32]{0:T(128)} %constant.216) | copy-start | bytes 388
  14.5 56.7 %reduce-scatter.6.cloned.1.call-start = ((), (), s32[]{:S(2)}) async-start(), calls=%async_computation.3 | async-start | bytes 327680 | tf_op jit(solution)/shard_map/while/body/eval_jaxpr/reduce_scatter | solution.py:115
  14.6 9.7 %collective-permute-start = (bf16[16,1024]{1,0:T(8,128)(2,1)S(1)}, bf16[16,1024]{1,0:T(8,128)(2,1)S(1)}, u32[]{:S(2)}, u32[]{:S(2)}) collective-permute-start(bf16[16,1024]{1,0:T(8,128)(2,1)S(1)} %broadcast_select_fusion.3), channel_id=1, source_target_pairs={{0,4},{4,8},{8,12},{1,5},{5,9},{9,13},{2,6},{6,10},{10,14},{3,7},{... | collective-permute-start | bytes 98312 | tf_op jit(solution)/shard_map/while/body/eval_jaxpr/ppermute | solution.py:28
  24.4 3.3 collective-permute-start.1
  27.7 3.3 collective-permute-start.2
  31.1 3.3 collective-permute-start.3
  34.4 10.2 %copy-start.1 = (f32[1,8,1024]{2,1,0:T(8,128)S(1)}, f32[1,8,1024]{2,1,0:T(8,128)}, u32[]{:S(2)}) copy-start(f32[1,8,1024]{2,1,0:T(8,128)} %get-tuple-element.621) | copy-start | bytes 98308 | tf_op jit(solution)/shard_map/while
  34.4 10.2 %copy-start.2 = (f32[8,1024]{1,0:T(8,128)S(1)}, f32[8,1024]{1,0:T(8,128)}, u32[]{:S(2)}) copy-start(f32[8,1024]{1,0:T(8,128)} %get-tuple-element.622) | copy-start | bytes 98308 | tf_op jit(solution)/shard_map/while
  72.1 54.0 %reduce-scatter.6.cloned.1.call-start = ((), (), s32[]{:S(2)}) async-start(), calls=%async_computation.3 | async-start | bytes 327680 | tf_op jit(solution)/shard_map/while/body/eval_jaxpr/reduce_scatter | solution.py:115
  72.1 8.2 %collective-permute-start = (bf16[16,1024]{1,0:T(8,128)(2,1)S(1)}, bf16[16,1024]{1,0:T(8,128)(2,1)S(1)}, u32[]{:S(2)}, u32[]{:S(2)}) collective-permute-start(bf16[16,1024]{1,0:T(8,128)(2,1)S(1)} %broadcast_select_fusion.3), channel_id=1, source_target_pairs={{0,4},{4,8},{8,12},{1,5},{5,9},{9,13},{2,6},{6,10},{10,14},{3,7},{... | collective-permute-start | bytes 98312 | tf_op jit(solution)/shard_map/while/body/eval_jaxpr/ppermute | solution.py:28
  80.4 3.3 collective-permute-start.1
  83.7 3.3 collective-permute-start.2
  87.1 3.3 collective-permute-start.3
  90.4 10.2 %copy-start.1 = (f32[1,8,1024]{2,1,0:T(8,128)S(1)}, f32[1,8,1024]{2,1,0:T(8,128)}, u32[]{:S(2)}) copy-start(f32[1,8,1024]{2,1,0:T(8,128)} %get-tuple-element.621) | copy-start | bytes 98308 | tf_op jit(solution)/shard_map/while
  90.4 10.2 %copy-start.2 = (f32[8,1024]{1,0:T(8,128)S(1)}, f32[8,1024]{1,0:T(8,128)}, u32[]{:S(2)}) copy-start(f32[8,1024]{1,0:T(8,128)} %get-tuple-element.622) | copy-start | bytes 98308 | tf_op jit(solution)/shard_map/while
  126.9 54.0 %reduce-scatter.6.cloned.1.call-start = ((), (), s32[]{:S(2)}) async-start(), calls=%async_computation.3 | async-start | bytes 327680 | tf_op jit(solution)/shard_map/while/body/eval_jaxpr/reduce_scatter | solution.py:115
  127.0 8.2 %collective-permute-start = (bf16[16,1024]{1,0:T(8,128)(2,1)S(1)}, bf16[16,1024]{1,0:T(8,128)(2,1)S(1)}, u32[]{:S(2)}, u32[]{:S(2)}) collective-permute-start(bf16[16,1024]{1,0:T(8,128)(2,1)S(1)} %broadcast_select_fusion.3), channel_id=1, source_target_pairs={{0,4},{4,8},{8,12},{1,5},{5,9},{9,13},{2,6},{6,10},{10,14},{3,7},{... | collective-permute-start | bytes 98312 | tf_op jit(solution)/shard_map/while/body/eval_jaxpr/ppermute | solution.py:28
  135.3 3.3 collective-permute-start.1
  138.6 3.3 collective-permute-start.2
  141.9 3.3 collective-permute-start.3
  145.3 10.2 %copy-start.2 = (f32[8,1024]{1,0:T(8,128)S(1)}, f32[8,1024]{1,0:T(8,128)}, u32[]{:S(2)}) copy-start(f32[8,1024]{1,0:T(8,128)} %get-tuple-element.622) | copy-start | bytes 98308 | tf_op jit(solution)/shard_map/while
  181.8 54.0 %reduce-scatter.6.cloned.1.call-start = ((), (), s32[]{:S(2)}) async-start(), calls=%async_computation.3 | async-start | bytes 327680 | tf_op jit(solution)/shard_map/while/body/eval_jaxpr/reduce_scatter | solution.py:115
  181.8 8.2 %collective-permute-start = (bf16[16,1024]{1,0:T(8,128)(2,1)S(1)}, bf16[16,1024]{1,0:T(8,128)(2,1)S(1)}, u32[]{:S(2)}, u32[]{:S(2)}) collective-permute-start(bf16[16,1024]{1,0:T(8,128)(2,1)S(1)} %broadcast_select_fusion.3), channel_id=1, source_target_pairs={{0,4},{4,8},{8,12},{1,5},{5,9},{9,13},{2,6},{6,10},{10,14},{3,7},{... | collective-permute-start | bytes 98312 | tf_op jit(solution)/shard_map/while/body/eval_jaxpr/ppermute | solution.py:28
  190.1 3.3 collective-permute-start.1
  193.5 3.3 collective-permute-start.2
  196.8 3.3 collective-permute-start.3
  200.1 10.2 %copy-start.2 = (f32[8,1024]{1,0:T(8,128)S(1)}, f32[8,1024]{1,0:T(8,128)}, u32[]{:S(2)}) copy-start(f32[8,1024]{1,0:T(8,128)} %get-tuple-element.622) | copy-start | bytes 98308 | tf_op jit(solution)/shard_map/while
  236.6 54.0 %reduce-scatter.6.cloned.1.call-start = ((), (), s32[]{:S(2)}) async-start(), calls=%async_computation.3 | async-start | bytes 327680 | tf_op jit(solution)/shard_map/while/body/eval_jaxpr/reduce_scatter | solution.py:115
  236.7 8.2 %collective-permute-start = (bf16[16,1024]{1,0:T(8,128)(2,1)S(1)}, bf16[16,1024]{1,0:T(8,128)(2,1)S(1)}, u32[]{:S(2)}, u32[]{:S(2)}) collective-permute-start(bf16[16,1024]{1,0:T(8,128)(2,1)S(1)} %broadcast_select_fusion.3), channel_id=1, source_target_pairs={{0,4},{4,8},{8,12},{1,5},{5,9},{9,13},{2,6},{6,10},{10,14},{3,7},{... | collective-permute-start | bytes 98312 | tf_op jit(solution)/shard_map/while/body/eval_jaxpr/ppermute | solution.py:28
  245.0 3.3 collective-permute-start.1
  248.3 3.3 collective-permute-start.2
  251.6 3.3 collective-permute-start.3
  255.0 10.2 %copy-start.2 = (f32[8,1024]{1,0:T(8,128)S(1)}, f32[8,1024]{1,0:T(8,128)}, u32[]{:S(2)}) copy-start(f32[8,1024]{1,0:T(8,128)} %get-tuple-element.622) | copy-start | bytes 98308 | tf_op jit(solution)/shard_map/while
  291.5 54.0 %reduce-scatter.6.cloned.1.call-start = ((), (), s32[]{:S(2)}) async-start(), calls=%async_computation.3 | async-start | bytes 327680 | tf_op jit(solution)/shard_map/while/body/eval_jaxpr/reduce_scatter | solution.py:115
  291.6 8.2 %collective-permute-start = (bf16[16,1024]{1,0:T(8,128)(2,1)S(1)}, bf16[16,1024]{1,0:T(8,128)(2,1)S(1)}, u32[]{:S(2)}, u32[]{:S(2)}) collective-permute-start(bf16[16,1024]{1,0:T(8,128)(2,1)S(1)} %broadcast_select_fusion.3), channel_id=1, source_target_pairs={{0,4},{4,8},{8,12},{1,5},{5,9},{9,13},{2,6},{6,10},{10,14},{3,7},{... | collective-permute-start | bytes 98312 | tf_op jit(solution)/shard_map/while/body/eval_jaxpr/ppermute | solution.py:28
  299.8 3.3 collective-permute-start.1
  303.2 3.3 collective-permute-start.2
  306.5 3.3 collective-permute-start.3
  309.8 10.2 %copy-start.2 = (f32[8,1024]{1,0:T(8,128)S(1)}, f32[8,1024]{1,0:T(8,128)}, u32[]{:S(2)}) copy-start(f32[8,1024]{1,0:T(8,128)} %get-tuple-element.622) | copy-start | bytes 98308 | tf_op jit(solution)/shard_map/while
  346.3 54.0 %reduce-scatter.6.cloned.1.call-start = ((), (), s32[]{:S(2)}) async-start(), calls=%async_computation.3 | async-start | bytes 327680 | tf_op jit(solution)/shard_map/while/body/eval_jaxpr/reduce_scatter | solution.py:115
  346.4 8.2 %collective-permute-start = (bf16[16,1024]{1,0:T(8,128)(2,1)S(1)}, bf16[16,1024]{1,0:T(8,128)(2,1)S(1)}, u32[]{:S(2)}, u32[]{:S(2)}) collective-permute-start(bf16[16,1024]{1,0:T(8,128)(2,1)S(1)} %broadcast_select_fusion.3), channel_id=1, source_target_pairs={{0,4},{4,8},{8,12},{1,5},{5,9},{9,13},{2,6},{6,10},{10,14},{3,7},{... | collective-permute-start | bytes 98312 | tf_op jit(solution)/shard_map/while/body/eval_jaxpr/ppermute | solution.py:28
  354.7 3.3 collective-permute-start.1
  358.0 3.3 collective-permute-start.2
  361.4 3.3 collective-permute-start.3
  364.7 10.2 %copy-start.2 = (f32[8,1024]{1,0:T(8,128)S(1)}, f32[8,1024]{1,0:T(8,128)}, u32[]{:S(2)}) copy-start(f32[8,1024]{1,0:T(8,128)} %get-tuple-element.622) | copy-start | bytes 98308 | tf_op jit(solution)/shard_map/while
  401.2 30.7 %reduce-scatter.4.cloned.1.call-start = ((), (), s32[]{:S(2)}) async-start(), calls=%async_computation.2 | async-start | bytes 40960 | tf_op jit(solution)/shard_map/reduce_scatter | solution.py:150
  (5 other events, 51.2 us)
Sparse Core Ops, SparseCore 0:
  50.9 20.2 reduce-scatter.5
  106.9 19.1 reduce-scatter.5
  161.7 19.1 reduce-scatter.5
  216.6 19.1 reduce-scatter.5
  271.4 19.1 reduce-scatter.5
  326.3 19.1 reduce-scatter.5
  381.1 19.1 reduce-scatter.5
Sparse Core Ops, SparseCore 1:
  409.1 19.8 reduce-scatter.3
